TPU v7x, 512 devices: a whole 4x8x8 slice. The times are simulated.
512 devices in a mesh: batch: 128 (over x, z, y_hi), mp: 4 (over y_lo, core).
Axes of the slice: x: 4, y: 8 (y_hi: 4, y_lo: 2; y = y_hi * 2 + y_lo), z: 8, core: 2. Of those that a mesh axis runs over, the one named last changes fastest.
Arguments:
- query_hidden: bfloat16 [131072, 768], P(('batch', 'mp')), may hold values from -28 to 28
- passage_hidden: bfloat16 [655360, 768], P(('batch', 'mp')), may hold values from -28 to 28
- projection: bfloat16 [768, 128], replicated, may hold values from -0.21875 to 0.21875
- query_lengths: int32 [4096], P(('batch', 'mp')), may hold values from 8 to 32, as said below
- passage_lengths: int32 [5120], P(('batch', 'mp')), may hold values from 64 to 128, as said below
- positives: int32 [4096], P(('batch', 'mp')), may hold values from 0 to 9
Outputs:
- query_loss: float32 [4096], P(('batch', 'mp'))
- grad_query_hidden: bfloat16 [131072, 768], P(('batch', 'mp'))
- grad_passage_hidden: bfloat16 [655360, 768], P(('batch', 'mp'))
- grad_projection: float32 [768, 128], replicated
Inputs may be any that keep to these rules, and one draw needn't show every extreme that they name: `query_lengths`: the first query of each block of 8 queries has all 32 tokens. `passage_lengths`: the first passage of each block of 10 passages has all 128 tokens.
All inputs are finite; a program needn't handle non-finite values.
Results may differ from a plain program's by a relative error of at most 0.012.
The roundings to bfloat16 on the way count: a program that leaves them out, or rounds other values in their place, can miss the bound.
Values may be sent and summed in bfloat16 or wider, within the bound.
A program may use at most 64 MiB of HBM per device.

v0:
```python
import jax
import jax.numpy as jnp
from jax import lax
from jax.sharding import PartitionSpec as P

inner_scale = 128.0
outer_scale = 8.0
loss_scale = 32.0
norm_eps = 1e-06


def shifted(block, axis, distance):
    devices = range(lax.axis_size(axis))
    route = [((i - distance) % len(devices), i) for i in devices]
    return lax.ppermute(block, axis, route)


def embed_rows(hidden, projection):
    before = jnp.dot(hidden, projection, preferred_element_type=jnp.float32)
    radius = jnp.sqrt(jnp.sum(before * before, axis=-1, keepdims=True) + norm_eps)
    return (before / radius, radius)


def candidate_block(query_embed, passage_embed, passage_valid, query_keep):
    queries, query_tokens = query_keep.shape
    passages, passage_tokens = passage_valid.shape
    sims = jnp.dot(query_embed, passage_embed.T, preferred_element_type=jnp.float32)
    sims = sims.reshape(queries, query_tokens, passages, passage_tokens)
    logits = jnp.where(passage_valid[None, None], sims * inner_scale, -jnp.inf)
    row_top = jnp.max(logits, axis=-1, keepdims=True)
    powers = jnp.exp(logits - row_top)
    totals = jnp.sum(powers, axis=-1, keepdims=True)
    weights = powers / totals
    best = (jnp.log(totals[..., 0]) + row_top[..., 0]) / inner_scale
    scores = outer_scale * jnp.sum(query_keep[:, :, None] * best, axis=1)
    return (scores, weights)


def softmax_loss(scores, positives):
    row_top = jnp.max(scores, axis=1, keepdims=True)
    totals = jnp.sum(jnp.exp(scores - row_top), axis=1, keepdims=True)
    log_total = row_top + jnp.log(totals)
    probs = jnp.exp(scores - log_total)
    columns = jnp.arange(scores.shape[1], dtype=jnp.int32)
    onehot = (columns[None, :] == positives[:, None]).astype(jnp.float32)
    losses = log_total[:, 0] - jnp.sum(onehot * scores, axis=1)
    return (losses, loss_scale * (probs - onehot))


def block_grads(dscores, query_keep, weights, query_embed, passage_embed):
    grad_sim = (
        outer_scale * dscores[:, None, :, None] * query_keep[:, :, None, None] * weights
    ).astype(jnp.bfloat16)
    flat = grad_sim.reshape(query_embed.shape[0], passage_embed.shape[0])
    to_query = jnp.dot(flat, passage_embed, preferred_element_type=jnp.float32)
    to_passage = lax.dot_general(
        flat, query_embed, (((0,), (0,)), ((), ())), preferred_element_type=jnp.float32
    )
    return (to_query, to_passage)


def back_norm(grad, unit, radius):
    return ((grad - unit * jnp.sum(unit * grad, axis=-1, keepdims=True)) / radius).astype(
        jnp.bfloat16
    )


def contract_rows(left, right):
    return lax.dot_general(
        left, right, (((0,), (0,)), ((), ())), preferred_element_type=jnp.float32
    )


def per_device(query_hidden, passage_hidden, projection, query_lengths, passage_lengths, positives):
    queries = query_lengths.shape[0]
    passages = passage_lengths.shape[0]
    query_tokens = query_hidden.shape[0] // queries
    passage_tokens = passage_hidden.shape[0] // passages
    query_unit, query_radius = embed_rows(query_hidden, projection)
    passage_unit, passage_radius = embed_rows(passage_hidden, projection)
    query_embed = query_unit.astype(jnp.bfloat16)
    passage_embed = passage_unit.astype(jnp.bfloat16)
    length_values = passage_lengths.astype(jnp.bfloat16)
    query_keep = (
        jnp.arange(query_tokens, dtype=jnp.int32)[None, :] < query_lengths[:, None]
    ).astype(jnp.float32)
    slots = jnp.arange(passage_tokens, dtype=jnp.float32)
    members = [(passage_embed, length_values)]
    current = (passage_embed, length_values)
    for repeat in range(2):
        current = shifted((current[0], current[1]), "batch", -1)
        members.append(current)
    score_list = []
    weight_list = []
    for member in members:
        valid = slots[None, :] < member[1].astype(jnp.float32)[:, None]
        scores, weights = candidate_block(query_embed, member[0], valid, query_keep)
        score_list.append(scores)
        weight_list.append(weights)
    losses, dscores = softmax_loss(jnp.concatenate(score_list, axis=1), positives)
    query_grad = jnp.zeros(query_unit.shape, jnp.float32)
    passage_terms = []
    for column in range(3):
        to_query, to_passage = block_grads(
            dscores[:, column * passages : (column + 1) * passages],
            query_keep,
            weight_list[column],
            query_embed,
            members[column][0],
        )
        query_grad = query_grad + to_query
        passage_terms.append(to_passage)
    query_pre_grad = back_norm(query_grad, query_unit, query_radius)
    query_partial = contract_rows(query_hidden, query_pre_grad)
    carried = passage_terms[2]
    for repeat in range(2):
        carried = (
            shifted(carried.astype(jnp.bfloat16), "batch", 1).astype(carried.dtype)
            + passage_terms[1 - repeat]
        )
    passage_pre_grad = back_norm(carried, passage_unit, passage_radius)
    grad_query_hidden = jnp.dot(
        query_pre_grad, projection.T, preferred_element_type=jnp.float32
    ).astype(jnp.bfloat16)
    grad_passage_hidden = jnp.dot(
        passage_pre_grad, projection.T, preferred_element_type=jnp.float32
    ).astype(jnp.bfloat16)
    passage_partial = contract_rows(passage_hidden, passage_pre_grad)
    weight_total = lax.psum(query_partial + passage_partial, ("batch", "mp"))
    grad_projection = weight_total / (lax.axis_size("batch") * lax.axis_size("mp"))
    return (losses, grad_query_hidden, grad_passage_hidden, grad_projection)


def solution(mesh):
    in_specs = (
        P(("batch", "mp"), None),
        P(("batch", "mp"), None),
        P(),
        P(("batch", "mp")),
        P(("batch", "mp")),
        P(("batch", "mp")),
    )
    out_specs = (P(("batch", "mp")), P(("batch", "mp"), None), P(("batch", "mp"), None), P())
    return jax.shard_map(
        per_device, mesh=mesh, in_specs=in_specs, out_specs=out_specs, check_vma=False
    )
```

profile of v0, /device:TPU:1, one launch (start us, length us, event | category | flops | bytes accessed | tf_op | source)
XLA Modules:
  0.0 411.5 jit_solution(9129074453687419694)
XLA Ops:
  7.3 1.5 copy-done
  8.7 1.7 multiply_reduce_fusion.1
  11.4 17.4 %collective-permute-start.1 = (bf16[1280,128]{0,1:T(8,128)(2,1)}, bf16[1280,128]{0,1:T(8,128)(2,1)}, u32[]{:S(2)}, u32[]{:S(2)}) collective-permute-start(bf16[1280,128]{0,1:T(8,128)(2,1)} %fusion.16), channel_id=1, source_target_pairs={{4,0},{8,4},{12,8},{16,12},{20,16},{24,20},{28,24},{32,28},{36,32}... | collective-permute-start | bytes 983048 | tf_op jit(solution)/shard_map/ppermute | solution.py:15
  29.3 3.8 collective-permute-start
  36.1 1.3 convolution_multiply_fusion.2
  37.5 1.6 mul.189
  39.0 2.4 select_reduce_fusion.2
  41.4 2.0 exponential_reduce_fusion.2
  45.4 9.0 %collective-permute-start.2 = (bf16[10]{0:T(256)(128)(2,1)}, bf16[10]{0:T(256)(128)(2,1)S(1)}, u32[]{:S(2)}, u32[]{:S(2)}) collective-permute-start(bf16[10]{0:T(256)(128)(2,1)} %collective-permute-done), channel_id=1, source_target_pairs={{4,0},{8,4},{12,8},{16,12},{20,16},{24,20},{28,24},{32,28},{36,32}... | collective-permute-start | bytes 68 | tf_op jit(solution)/shard_map/ppermute | solution.py:15
  55.9 2.4 convolution_multiply_fusion.1
  58.3 2.7 mul.196
  60.9 10.2 %collective-permute-start.3 = (bf16[1280,128]{0,1:T(8,128)(2,1)}, bf16[1280,128]{0,1:T(8,128)(2,1)S(1)}, u32[]{:S(2)}, u32[]{:S(2)}) collective-permute-start(bf16[1280,128]{0,1:T(8,128)(2,1)} %collective-permute-done.1), channel_id=1, source_target_pairs={{4,0},{8,4},{12,8},{16,12},{20,16},{24,20},{28,24},{32,28},{36,32}... | collective-permute-start | bytes 983048 | tf_op jit(solution)/shard_map/ppermute | solution.py:15
  71.2 2.2 select_reduce_fusion.1
  73.4 1.9 exponential_reduce_fusion.1
  75.4 1.1 collective-permute-done.3
  77.2 1.4 convolution_multiply_fusion
  78.7 2.7 mul.200
  81.3 2.4 select_reduce_fusion
  83.7 1.3 exponential_reduce_fusion
  88.4 2.0 fusion.7
  90.4 1.3 fusion.18
  93.7 2.0 fusion.1
  95.9 3.1 collective-permute-start.4
  100.9 2.0 fusion.4
  102.9 1.3 convolution_add_fusion.2
  104.8 5.4 %collective-permute-done.4 = bf16[1280,128]{0,1:T(8,128)(2,1)S(1)} collective-permute-done((bf16[1280,128]{0,1:T(8,128)(2,1)S(1)}, bf16[1280,128]{0,1:T(8,128)(2,1)S(1)}, u32[]{:S(2)}, u32[]{:S(2)}) %collective-permute-start.4) | collective-permute-done | bytes 327712 | tf_op jit(solution)/shard_map/ppermute | solution.py:15
  110.4 1.9 collective-permute-start.5
  112.3 1.0 convolution_convert_fusion.2
  113.6 13.6 %collective-permute-done.5 = bf16[1280,128]{0,1:T(8,128)(2,1)S(1)} collective-permute-done((bf16[1280,128]{0,1:T(8,128)(2,1)S(1)}, bf16[1280,128]{0,1:T(8,128)(2,1)S(1)}, u32[]{:S(2)}, u32[]{:S(2)}) %collective-permute-start.5) | collective-permute-done | bytes 327712 | tf_op jit(solution)/shard_map/ppermute | solution.py:15
  127.6 1.2 fusion.9
  128.8 2.0 convolution_convert_fusion
  130.8 271.9 %all-reduce.2.cloned.1.call-done = f32[768,128]{0,1:T(8,128)} async-done(((f32[768,128]{0,1:T(8,128)}), f32[768,128]{0,1:T(8,128)}) %all-reduce.2.cloned.1.call-update) | async-done | bytes 393232 | tf_op jit(solution)/shard_map/psum | solution.py:129
  (114 shorter events, 19.2 us)
Async XLA Ops:
  7.2 1.6 copy-start
  7.2 27.9 %copy-start.8 = (bf16[768,128]{1,0:T(8,128)(2,1)S(1)}, bf16[768,128]{1,0:T(8,128)(2,1)}, u32[]{:S(2)}) copy-start(bf16[768,128]{1,0:T(8,128)(2,1)} %param.8) | copy-start | bytes 589828
  7.2 21.6 %copy-start.31 = (s32[10]{0:T(128)S(1)}, s32[10]{0:T(128)}, u32[]{:S(2)}) copy-start(s32[10]{0:T(128)} %param.10) | copy-start | bytes 124
  7.2 25.8 %copy-start.29 = (s32[8]{0:T(128)S(1)}, s32[8]{0:T(128)}, u32[]{:S(2)}) copy-start(s32[8]{0:T(128)} %param.9) | copy-start | bytes 100
  7.2 27.9 %copy-start.13 = (bf16[256,768]{1,0:T(8,128)(2,1)S(1)}, bf16[256,768]{1,0:T(8,128)(2,1)}, u32[]{:S(2)}) copy-start(bf16[256,768]{1,0:T(8,128)(2,1)} %param.6) | copy-start | bytes 1179652
  7.2 395.5 %all-reduce.2.cloned.1.call-start = ((), (), s32[]{:S(2)}) async-start(), calls=%async_computation | async-start | bytes 786432 | tf_op jit(solution)/shard_map/psum | solution.py:129
  10.5 25.0 %copy-start.6 = (f32[1280,128]{0,1:T(8,128)}, f32[1280,128]{0,1:T(8,128)S(1)}, u32[]{:S(2)}) copy-start(f32[1280,128]{0,1:T(8,128)S(1)} %get-tuple-element.37) | copy-start | bytes 1966084
  11.4 44.5 %collective-permute-start.1 = (bf16[1280,128]{0,1:T(8,128)(2,1)}, bf16[1280,128]{0,1:T(8,128)(2,1)}, u32[]{:S(2)}, u32[]{:S(2)}) collective-permute-start(bf16[1280,128]{0,1:T(8,128)(2,1)} %fusion.16), channel_id=1, source_target_pairs={{4,0},{8,4},{12,8},{16,12},{20,16},{24,20},{28,24},{32,28},{36,32}... | collective-permute-start | bytes 983048 | tf_op jit(solution)/shard_map/ppermute | solution.py:15
  29.3 14.7 %collective-permute-start = (bf16[10]{0:T(256)(128)(2,1)}, bf16[10]{0:T(256)(128)(2,1)}, u32[]{:S(2)}, u32[]{:S(2)}) collective-permute-start(bf16[10]{0:T(256)(128)(2,1)} %get-tuple-element.33), channel_id=1, source_target_pairs={{4,0},{8,4},{12,8},{16,12},{20,16},{24,20},{28,24},{32,28},{36,32}... | collective-permute-start | bytes 68 | tf_op jit(solution)/shard_map/ppermute | solution.py:15
  39.0 2.4 copy-start.2
  39.0 2.4 copy-start.21
  41.4 2.0 copy-start.9
  45.4 9.8 %collective-permute-start.2 = (bf16[10]{0:T(256)(128)(2,1)}, bf16[10]{0:T(256)(128)(2,1)S(1)}, u32[]{:S(2)}, u32[]{:S(2)}) collective-permute-start(bf16[10]{0:T(256)(128)(2,1)} %collective-permute-done), channel_id=1, source_target_pairs={{4,0},{8,4},{12,8},{16,12},{20,16},{24,20},{28,24},{32,28},{36,32}... | collective-permute-start | bytes 68 | tf_op jit(solution)/shard_map/ppermute | solution.py:15
  60.9 12.5 %copy-start.1 = (f32[8,32,10,128]{3,2,1,0:T(8,128)S(1)}, f32[8,32,10,128]{3,2,1,0:T(8,128)}, u32[]{:S(2)}) copy-start(f32[8,32,10,128]{3,2,1,0:T(8,128)} %mul.196) | copy-start | bytes 3932164
  60.9 15.6 %collective-permute-start.3 = (bf16[1280,128]{0,1:T(8,128)(2,1)}, bf16[1280,128]{0,1:T(8,128)(2,1)S(1)}, u32[]{:S(2)}, u32[]{:S(2)}) collective-permute-start(bf16[1280,128]{0,1:T(8,128)(2,1)} %collective-permute-done.1), channel_id=1, source_target_pairs={{4,0},{8,4},{12,8},{16,12},{20,16},{24,20},{28,24},{32,28},{36,32}... | collective-permute-start | bytes 983048 | tf_op jit(solution)/shard_map/ppermute | solution.py:15
  73.4 2.0 copy-start.11
  81.3 2.4 copy-start.3
  81.3 3.7 copy-start.10
  81.3 3.8 copy-start.12
  81.3 3.8 copy-start.17
  81.3 3.8 copy-start.18
  81.3 3.8 copy-start.23
  83.7 1.8 copy-start.30
  83.7 2.7 copy-start.22
  95.9 14.2 %collective-permute-start.4 = (bf16[1280,128]{0,1:T(8,128)(2,1)S(1)}, bf16[1280,128]{0,1:T(8,128)(2,1)S(1)}, u32[]{:S(2)}, u32[]{:S(2)}) collective-permute-start(bf16[1280,128]{0,1:T(8,128)(2,1)S(1)} %convolution_convert_fusion.1), channel_id=1, source_target_pairs={{508,0},{0,4},{4,8},{8,12},{12,16},{16,20},{20,24},{24,28},{28,32}... | collective-permute-start | bytes 983048 | tf_op jit(solution)/shard_map/ppermute | solution.py:15
  99.6 1.3 copy-start.4
  100.9 3.4 copy-start.16
  100.9 3.4 copy-start.20
  100.9 3.4 copy-start.25
  104.3 9.1 %copy-start.14 = (bf16[256,768]{1,0:T(8,128)(2,1)S(1)}, bf16[256,768]{1,0:T(8,128)(2,1)}, u32[]{:S(2)}) copy-start(bf16[256,768]{1,0:T(8,128)(2,1)} %param.6) | copy-start | bytes 1179652
  104.3 22.9 %copy-start.7 = (f32[1280,128]{0,1:T(8,128)S(1)}, f32[1280,128]{0,1:T(8,128)}, u32[]{:S(2)}) copy-start(f32[1280,128]{0,1:T(8,128)} %copy-done.6) | copy-start | bytes 1966084
  110.4 16.8 %collective-permute-start.5 = (bf16[1280,128]{0,1:T(8,128)(2,1)S(1)}, bf16[1280,128]{0,1:T(8,128)(2,1)S(1)}, u32[]{:S(2)}, u32[]{:S(2)}) collective-permute-start(bf16[1280,128]{0,1:T(8,128)(2,1)S(1)} %add_convert_fusion), channel_id=1, source_target_pairs={{508,0},{0,4},{4,8},{8,12},{12,16},{16,20},{20,24},{24,28},{28,32}... | collective-permute-start | bytes 983048 | tf_op jit(solution)/shard_map/ppermute | solution.py:15
  (7 other events, 7.2 us)
Sparse Core Ops, SparseCore 0:
  129.0 273.7 all-reduce.1
where the time goes:
time: 412 us
  waiting for transfers between devices  293 us (71%)
  starting transfers between devices  45.4 us (11%)
  other arithmetic  26.7 us (6%)
  local copies, waits for them, and re-layouts  16.6 us (4%)
  matrix products  15.4 us (4%)
  between operations  14.7 us (4%)
    psum x1, waiting for transfers between devices, per_device(): weight_total = lax.psum(query_partial + passage_partial, ('batch', 'mp'))  272 us
    ppermute x6, starting transfers between devices, shifted(): return lax.ppermute(block, axis, route)  45.3 us
    ppermute x6, waiting for transfers between devices, shifted(): return lax.ppermute(block, axis, route)  20.9 us
  transfers between devices with their start and end apart: 7, of which 5 were waited for; matrix products, arithmetic and copies ran while one was open for 6% of the time, Pallas kernels for 0%

commit v1 on v0

--- a/solution.py
+++ b/solution.py
@@ -126,7 +126,9 @@
         passage_pre_grad, projection.T, preferred_element_type=jnp.float32
     ).astype(jnp.bfloat16)
     passage_partial = contract_rows(passage_hidden, passage_pre_grad)
-    weight_total = lax.psum(query_partial + passage_partial, ("batch", "mp"))
+    weight_total = query_partial + passage_partial
+    for name in ("mp", "batch"):
+        weight_total = lax.psum(weight_total, name)
     grad_projection = weight_total / (lax.axis_size("batch") * lax.axis_size("mp"))
     return (losses, grad_query_hidden, grad_passage_hidden, grad_projection)
 

time: 412 us -> 1520 us (3.69)
  the two profiles are of different devices: /device:TPU:1 before, /device:TPU:16 now
where the time goes in v1:
time: 1520 us
  waiting for transfers between devices  1410 us (93%)
  starting transfers between devices  36.9 us (2%)
  other arithmetic  26.7 us (2%)
  local copies, waits for them, and re-layouts  16.6 us (1%)
  matrix products  15.5 us (1%)
    psum x2, waiting for transfers between devices, per_device(): weight_total = lax.psum(weight_total, name)  1370 us
    ppermute x6, starting transfers between devices, shifted(): return lax.ppermute(block, axis, route)  36.9 us
    ppermute x6, waiting for transfers between devices, shifted(): return lax.ppermute(block, axis, route)  36 us
  transfers between devices with their start and end apart: 8, of which 6 were waited for; matrix products, arithmetic and copies ran while one was open for 2% of the time, Pallas kernels for 0%

profile of v1, /device:TPU:16, one launch (start us, length us, event | category | flops | bytes accessed | tf_op | source)
XLA Modules:
  0.0 1517.7 jit_solution(17414189656046952177)
XLA Ops:
  7.3 1.5 copy-done
  8.7 1.7 multiply_reduce_fusion.1
  11.4 7.6 collective-permute-start.1
  19.5 11.5 collective-permute-start
  34.1 1.3 convolution_multiply_fusion.2
  35.4 1.6 mul.189
  37.0 2.4 select_reduce_fusion.2
  39.4 2.0 exponential_reduce_fusion.2
  43.3 4.0 collective-permute-start.2
  47.4 3.7 collective-permute-done.2
  51.9 2.4 convolution_multiply_fusion.1
  54.2 2.7 mul.196
  56.9 7.6 collective-permute-start.3
  64.5 2.2 select_reduce_fusion.1
  66.8 1.9 exponential_reduce_fusion.1
  68.7 5.5 collective-permute-done.3
  75.0 1.4 convolution_multiply_fusion
  76.4 2.7 mul.200
  79.1 2.4 select_reduce_fusion
  81.5 1.3 exponential_reduce_fusion
  86.1 2.0 fusion.7
  88.1 1.3 fusion.18
  91.4 2.0 fusion.1
  93.7 2.6 collective-permute-start.4
  98.2 2.0 fusion.4
  100.3 1.4 convolution_add_fusion.2
  102.1 7.9 collective-permute-done.4
  110.3 3.5 collective-permute-start.5
  114.1 18.8 %collective-permute-done.5 = bf16[1280,128]{0,1:T(8,128)(2,1)S(1)} collective-permute-done((bf16[1280,128]{0,1:T(8,128)(2,1)S(1)}, bf16[1280,128]{0,1:T(8,128)(2,1)S(1)}, u32[]{:S(2)}, u32[]{:S(2)}) %collective-permute-start.5) | collective-permute-done | bytes 327712 | tf_op jit(solution)/shard_map/ppermute | solution.py:15
  134.6 44.1 %all-reduce.3.cloned.1.call-done = f32[768,128]{0,1:T(8,128)} async-done(((f32[768,128]{0,1:T(8,128)}), f32[768,128]{0,1:T(8,128)}) %all-reduce.3.cloned.1.call-update) | async-done | bytes 393232 | tf_op jit(solution)/shard_map/psum | solution.py:131
  179.8 2.0 convolution_convert_fusion
  181.8 1327.2 %all-reduce.5.cloned.1.call-done = f32[768,128]{0,1:T(8,128)} async-done(((f32[768,128]{0,1:T(8,128)}), f32[768,128]{0,1:T(8,128)}) %all-reduce.5.cloned.1.call-update) | async-done | bytes 393232 | tf_op jit(solution)/shard_map/psum | solution.py:131
  (117 shorter events, 20.8 us)
Async XLA Ops:
  7.2 1.6 copy-start
  7.2 25.9 %copy-start.8 = (bf16[768,128]{1,0:T(8,128)(2,1)S(1)}, bf16[768,128]{1,0:T(8,128)(2,1)}, u32[]{:S(2)}) copy-start(bf16[768,128]{1,0:T(8,128)(2,1)} %param.8) | copy-start | bytes 589828
  7.2 11.8 copy-start.31
  7.2 23.8 %copy-start.29 = (s32[8]{0:T(128)S(1)}, s32[8]{0:T(128)}, u32[]{:S(2)}) copy-start(s32[8]{0:T(128)} %param.9) | copy-start | bytes 100
  7.2 25.9 %copy-start.13 = (bf16[256,768]{1,0:T(8,128)(2,1)S(1)}, bf16[256,768]{1,0:T(8,128)(2,1)}, u32[]{:S(2)}) copy-start(bf16[256,768]{1,0:T(8,128)(2,1)} %param.6) | copy-start | bytes 1179652
  7.2 171.5 %all-reduce.3.cloned.1.call-start = ((), (), s32[]{:S(2)}) async-start(), calls=%async_computation | async-start | bytes 786432 | tf_op jit(solution)/shard_map/psum | solution.py:131
  10.5 22.9 %copy-start.6 = (f32[1280,128]{0,1:T(8,128)}, f32[1280,128]{0,1:T(8,128)S(1)}, u32[]{:S(2)}) copy-start(f32[1280,128]{0,1:T(8,128)S(1)} %get-tuple-element.37) | copy-start | bytes 1966084
  11.4 40.5 %collective-permute-start.1 = (bf16[1280,128]{0,1:T(8,128)(2,1)}, bf16[1280,128]{0,1:T(8,128)(2,1)}, u32[]{:S(2)}, u32[]{:S(2)}) collective-permute-start(bf16[1280,128]{0,1:T(8,128)(2,1)} %fusion.16), channel_id=1, source_target_pairs={{4,0},{8,4},{12,8},{16,12},{20,16},{24,20},{28,24},{32,28},{36,32}... | collective-permute-start | bytes 983048 | tf_op jit(solution)/shard_map/ppermute | solution.py:15
  19.5 22.4 %collective-permute-start = (bf16[10]{0:T(256)(128)(2,1)}, bf16[10]{0:T(256)(128)(2,1)}, u32[]{:S(2)}, u32[]{:S(2)}) collective-permute-start(bf16[10]{0:T(256)(128)(2,1)} %get-tuple-element.33), channel_id=1, source_target_pairs={{4,0},{8,4},{12,8},{16,12},{20,16},{24,20},{28,24},{32,28},{36,32}... | collective-permute-start | bytes 68 | tf_op jit(solution)/shard_map/ppermute | solution.py:15
  37.0 2.4 copy-start.2
  37.0 2.4 copy-start.21
  39.4 2.0 copy-start.9
  43.3 7.8 collective-permute-start.2
  56.9 9.9 copy-start.1
  56.9 17.4 %collective-permute-start.3 = (bf16[1280,128]{0,1:T(8,128)(2,1)}, bf16[1280,128]{0,1:T(8,128)(2,1)S(1)}, u32[]{:S(2)}, u32[]{:S(2)}) collective-permute-start(bf16[1280,128]{0,1:T(8,128)(2,1)} %collective-permute-done.1), channel_id=1, source_target_pairs={{4,0},{8,4},{12,8},{16,12},{20,16},{24,20},{28,24},{32,28},{36,32}... | collective-permute-start | bytes 983048 | tf_op jit(solution)/shard_map/ppermute | solution.py:15
  66.8 2.0 copy-start.11
  79.1 2.4 copy-start.3
  79.1 3.7 copy-start.10
  79.1 3.8 copy-start.12
  79.1 3.8 copy-start.17
  79.1 3.8 copy-start.18
  79.1 3.8 copy-start.23
  81.5 1.8 copy-start.30
  81.5 2.7 copy-start.22
  93.7 16.3 %collective-permute-start.4 = (bf16[1280,128]{0,1:T(8,128)(2,1)S(1)}, bf16[1280,128]{0,1:T(8,128)(2,1)S(1)}, u32[]{:S(2)}, u32[]{:S(2)}) collective-permute-start(bf16[1280,128]{0,1:T(8,128)(2,1)S(1)} %convolution_convert_fusion.1), channel_id=1, source_target_pairs={{508,0},{0,4},{4,8},{8,12},{12,16},{16,20},{20,24},{24,28},{28,32}... | collective-permute-start | bytes 983048 | tf_op jit(solution)/shard_map/ppermute | solution.py:15
  98.2 3.4 copy-start.16
  98.2 3.4 copy-start.20
  98.2 3.4 copy-start.25
  100.3 13.6 copy-start.14
  101.7 31.2 %copy-start.7 = (f32[1280,128]{0,1:T(8,128)S(1)}, f32[1280,128]{0,1:T(8,128)}, u32[]{:S(2)}) copy-start(f32[1280,128]{0,1:T(8,128)} %copy-done.6) | copy-start | bytes 1966084
  110.3 22.6 %collective-permute-start.5 = (bf16[1280,128]{0,1:T(8,128)(2,1)S(1)}, bf16[1280,128]{0,1:T(8,128)(2,1)S(1)}, u32[]{:S(2)}, u32[]{:S(2)}) collective-permute-start(bf16[1280,128]{0,1:T(8,128)(2,1)S(1)} %add_convert_fusion), channel_id=1, source_target_pairs={{508,0},{0,4},{4,8},{8,12},{12,16},{16,20},{20,24},{24,28},{28,32}... | collective-permute-start | bytes 983048 | tf_op jit(solution)/shard_map/ppermute | solution.py:15
  134.5 1374.4 %all-reduce.5.cloned.1.call-start = ((), (), s32[]{:S(2)}) async-start(), calls=%async_computation.1 | async-start | bytes 786432 | tf_op jit(solution)/shard_map/psum | solution.py:131
  (8 other events, 8.5 us)
Sparse Core Ops, SparseCore 0:
  134.7 44.0 all-reduce.2
  181.6 1327.2 all-reduce.4
